TPU v7x, 32 devices: a whole 2x2x4 slice. The times are simulated.
32 devices in a mesh: dp: 4 (over z), cent: 8 (over y, x, core).
Axes of the slice: x: 2, y: 2, z: 4, core: 2. Of those that a mesh axis runs over, the one named last changes fastest.
Arguments:
- vectors: bfloat16 [8192, 768], P('dp'), may hold values from -30 to 30
- centroids: bfloat16 [16384, 768], P('cent'), may hold values from -1 to 1
- assignment: int32 [8192], P(('dp', 'cent')), may hold values from 0 to 16383, as said below
Outputs:
- new_centroids: bfloat16 [16384, 768], P('cent')
- row_potential: float32 [8192], P('dp')
- column_potential: float32 [16384], P('cent')
- residuals: bfloat16 [8192, 768], P(('dp', 'cent'))
Inputs may be any that keep to these rules, and one draw needn't show every extreme that they name: `assignment`: the entry's centroid is owned by index entry // 2048 of cent. In each aligned block of 256 entries (the rows of one device), at most 64 entries name centroids of one owning index; one owning index, drawn from the seed, receives exactly 64 entries from every block.
All inputs are finite; a program needn't handle non-finite values.
Results may differ from a plain program's by a relative error of at most 0.00705.
Values may be sent and summed in bfloat16 or wider, within the bound.
No kernel may reach another device: no remote copies, remote signals or barrier semaphores. Data moves between devices by JAX's collectives and lax.ppermute only.
A program may use at most 128 MiB of HBM per device.

v0:
```python
import math
import jax
import jax.numpy as jnp
from jax import lax
from jax.sharding import PartitionSpec as P

ITERS = 3
inv_temp = 2.0


def merged(value, axis, join):
    pieces = jax.tree.map(lambda part: lax.all_gather(part, axis), value)
    head = jax.tree.map(lambda part: part[0], pieces)
    tail = jax.tree.map(lambda part: part[1:], pieces)
    so_far, _ = lax.scan(lambda so_far, slab: (join(so_far, slab), None), head, tail)
    return so_far


def combine_pair(earlier, later):
    highest = jnp.maximum(earlier[0], later[0])
    return (
        highest,
        earlier[1] * jnp.exp(earlier[0] - highest) + later[1] * jnp.exp(later[0] - highest),
    )


def local_pair(shifted, axis):
    highest = jnp.max(shifted, axis=axis)
    summed = jnp.sum(jnp.exp(shifted - jnp.expand_dims(highest, axis)), axis=axis)
    return (highest, summed)


def on_device(vectors, centroids, assignment):
    row_count = vectors.shape[0]
    list_count = centroids.shape[0]
    width = vectors.shape[1]
    data_count = lax.axis_size("dp")
    owner_count = lax.axis_size("cent")
    logits = inv_temp * lax.dot_general(
        vectors, centroids, (((1,), (1,)), ((), ())), preferred_element_type=jnp.float32
    )
    log_mass = math.log(row_count * data_count / (list_count * owner_count))
    row_shift = jnp.zeros((row_count,), jnp.float32)
    column_shift = jnp.zeros((list_count,), jnp.float32)
    for iteration in range(ITERS):
        column_peak, column_total = local_pair(logits + row_shift[:, None], 0)
        column_peak, column_total = merged((column_peak, column_total), "dp", combine_pair)
        column_shift = log_mass - (column_peak + jnp.log(column_total))
        shifted = logits + column_shift[None, :]
        row_peak = lax.pmax(jnp.max(shifted, axis=1), "cent")
        row_total = lax.psum(jnp.sum(jnp.exp(shifted - row_peak[:, None]), axis=1), "cent")
        row_shift = -(row_peak + jnp.log(row_total))
    weights = jnp.exp(logits + row_shift[:, None] + column_shift[None, :]).astype(jnp.bfloat16)
    numerator = lax.dot_general(
        weights, vectors, (((0,), (0,)), ((), ())), preferred_element_type=jnp.float32
    )
    mass = jnp.sum(weights.astype(jnp.float32), axis=0)
    share_numer, share_mass = (
        lax.psum_scatter(numerator, "dp", scatter_dimension=0, tiled=True),
        lax.psum_scatter(mass, "dp", scatter_dimension=0, tiled=True),
    )
    share_rows = (share_numer / share_mass[:, None]).astype(jnp.bfloat16)
    updated = lax.all_gather(share_rows, "dp", axis=0, tiled=True)
    send_count = row_count // owner_count
    capacity = max(2, 2 * send_count // owner_count)
    sender_rows = lax.dynamic_slice_in_dim(
        vectors, lax.axis_index("cent") * send_count, send_count, 0
    )
    targets = assignment // list_count
    local_ids = assignment % list_count
    positions = jnp.arange(send_count, dtype=jnp.int32)
    earlier_same = (targets[:, None] == targets[None, :]) & (
        positions[None, :] < positions[:, None]
    )
    ranks = jnp.sum(earlier_same.astype(jnp.int32), axis=1)
    slots = targets * capacity + ranks
    outgoing = jnp.zeros((owner_count * capacity, width), jnp.bfloat16).at[slots].set(sender_rows)
    outgoing_ids = jnp.zeros((owner_count * capacity,), jnp.int32).at[slots].set(local_ids)
    outgoing = outgoing.reshape(owner_count, capacity, width)
    outgoing_ids = outgoing_ids.reshape(owner_count, capacity)
    arrived = lax.all_to_all(outgoing, "cent", split_axis=0, concat_axis=0, tiled=True)
    arrived_ids = lax.all_to_all(outgoing_ids, "cent", split_axis=0, concat_axis=0, tiled=True)
    residual_rows = (arrived.astype(jnp.float32) - updated[arrived_ids].astype(jnp.float32)).astype(
        jnp.bfloat16
    )
    returned = lax.all_to_all(residual_rows, "cent", split_axis=0, concat_axis=0, tiled=True)
    residuals = returned.reshape(owner_count * capacity, width)[slots]
    return (updated, row_shift, column_shift, residuals)


def solution(mesh):
    in_specs = (P("dp", None), P("cent", None), P(("dp", "cent")))
    out_specs = (P("cent", None), P("dp"), P("cent"), P(("dp", "cent"), None))
    return jax.shard_map(
        on_device, mesh=mesh, in_specs=in_specs, out_specs=out_specs, check_vma=False
    )
```

profile of v0, /device:TPU:0, one launch (start us, length us, event | category | flops | bytes accessed | tf_op | source)
XLA Modules:
  0.0 489.4 jit_solution(13320636421728077944)
XLA Ops:
  9.1 11.5 %fusion.7 = (f32[2048]{0:T(1024)S(1)}, f32[2048,2048]{1,0:T(8,128)}) fusion(bf16[2048,768]{1,0:T(8,128)(2,1)S(1)} %copy-done, bf16[2048,768]{1,0:T(8,128)(2,1)} %param.10), kind=kOutput, calls=%fused_computation.55 | convolution fusion | flops 6450837504 | bytes 23076864 | tf_op jit(solution)/shard_map/dot_general | solution.py:39
  20.5 8.1 %exponential_reduce_fusion.5 = f32[2048]{0:T(1024)S(1)} fusion(f32[2048,2048]{1,0:T(8,128)} %get-tuple-element.141, f32[2048]{0:T(1024)S(1)} %get-tuple-element.140), kind=kLoop, calls=%fused_computation.20 | loop fusion | flops 8386560 | bytes 16793600 | tf_op jit(solution)/shard_map/reduce_sum | solution.py:29
  28.6 14.8 %all-gather.1 = f32[8192]{0:T(1024)S(1)} all-gather(f32[2048]{0:T(1024)S(1)} %exponential_reduce_fusion.5), channel_id=3, replica_groups=mesh['dp'=4,'cent'=8] {'dp'}, dimensions={0}, use_global_device_ids=true | all-gather | bytes 40960 | tf_op jit(solution)/shard_map/all_gather | solution.py:12
  43.5 13.2 %all-gather = f32[8192]{0:T(1024)S(1)} all-gather(f32[2048]{0:T(1024)S(1)} %get-tuple-element.140), channel_id=2, replica_groups=mesh['dp'=4,'cent'=8] {'dp'}, dimensions={0}, use_global_device_ids=true | all-gather | bytes 40960 | tf_op jit(solution)/shard_map/all_gather | solution.py:12
  63.8 12.1 %pmax.21 = f32[2048]{0:T(1024)S(1)} all-reduce(f32[2048]{0:T(1024)S(1)} %add_reduce_fusion.4), channel_id=1, replica_groups=mesh['dp'=4,'cent'=8] {'cent'}, use_global_device_ids=true, to_apply=%region_5.6 | all-reduce | flops 2048 | bytes 16384 | tf_op jit(solution)/shard_map/pmax | solution.py:50
  75.9 7.7 %exponential_reduce_fusion.4 = f32[2048]{0:T(1024)S(1)} fusion(f32[2048,2048]{1,0:T(8,128)} %get-tuple-element.141, f32[2048]{0:T(1024)S(1)} %pmax.21, f32[2048]{0:T(1024)S(1)} %add_subtract_fusion.2), kind=kLoop, calls=%fused_computation.19 | loop fusion | flops 12580864 | bytes 16801792 | tf_op jit(solution)/shard_map/reduce_sum | solution.py:51
  83.6 12.1 %psum.21 = f32[2048]{0:T(1024)S(1)} all-reduce(f32[2048]{0:T(1024)S(1)} %exponential_reduce_fusion.4), channel_id=1, replica_groups=mesh['dp'=4,'cent'=8] {'cent'}, use_global_device_ids=true, to_apply=%region_7.8 | all-reduce | flops 2048 | bytes 16384 | tf_op jit(solution)/shard_map/psum | solution.py:51
  102.6 7.6 %exponential_reduce_fusion.3 = f32[2048]{0:T(1024)S(1)} fusion(f32[2048,2048]{1,0:T(8,128)} %get-tuple-element.141, f32[2048]{0:T(1024)S(1)} %add_reduce_fusion.3, f32[2048]{0:T(1024)S(1)} %add_negate_fusion.2), kind=kLoop, calls=%fused_computation.18 | loop fusion | flops 12580864 | bytes 16801792 | tf_op jit(solution)/shard_map/reduce_sum | solution.py:29
  110.3 13.1 %all-gather.2 = f32[8192]{0:T(1024)S(1)} all-gather(f32[2048]{0:T(1024)S(1)} %add_reduce_fusion.3), channel_id=4, replica_groups=mesh['dp'=4,'cent'=8] {'dp'}, dimensions={0}, use_global_device_ids=true | all-gather | bytes 40960 | tf_op jit(solution)/shard_map/all_gather | solution.py:12
  123.4 13.2 %all-gather.3 = f32[8192]{0:T(1024)S(1)} all-gather(f32[2048]{0:T(1024)S(1)} %exponential_reduce_fusion.3), channel_id=5, replica_groups=mesh['dp'=4,'cent'=8] {'dp'}, dimensions={0}, use_global_device_ids=true | all-gather | bytes 40960 | tf_op jit(solution)/shard_map/all_gather | solution.py:12
  143.8 12.0 %pmax.22 = f32[2048]{0:T(1024)S(1)} all-reduce(f32[2048]{0:T(1024)S(1)} %add_reduce_fusion.2), channel_id=1, replica_groups=mesh['dp'=4,'cent'=8] {'cent'}, use_global_device_ids=true, to_apply=%region_13.14 | all-reduce | flops 2048 | bytes 16384 | tf_op jit(solution)/shard_map/pmax | solution.py:50
  155.8 7.7 %exponential_reduce_fusion.2 = f32[2048]{0:T(1024)S(1)} fusion(f32[2048,2048]{1,0:T(8,128)} %get-tuple-element.141, f32[2048]{0:T(1024)S(1)} %pmax.22, f32[2048]{0:T(1024)S(1)} %add_subtract_fusion.1), kind=kLoop, calls=%fused_computation.17 | loop fusion | flops 12580864 | bytes 16801792 | tf_op jit(solution)/shard_map/reduce_sum | solution.py:51
  163.5 12.2 %psum.22 = f32[2048]{0:T(1024)S(1)} all-reduce(f32[2048]{0:T(1024)S(1)} %exponential_reduce_fusion.2), channel_id=1, replica_groups=mesh['dp'=4,'cent'=8] {'cent'}, use_global_device_ids=true, to_apply=%region_15.16 | all-reduce | flops 2048 | bytes 16384 | tf_op jit(solution)/shard_map/psum | solution.py:51
  190.3 13.1 %all-gather.4 = f32[8192]{0:T(1024)S(1)} all-gather(f32[2048]{0:T(1024)S(1)} %add_reduce_fusion.1), channel_id=6, replica_groups=mesh['dp'=4,'cent'=8] {'dp'}, dimensions={0}, use_global_device_ids=true | all-gather | bytes 40960 | tf_op jit(solution)/shard_map/all_gather | solution.py:12
  203.4 13.2 %all-gather.5 = f32[8192]{0:T(1024)S(1)} all-gather(f32[2048]{0:T(1024)S(1)} %exponential_reduce_fusion.1), channel_id=7, replica_groups=mesh['dp'=4,'cent'=8] {'dp'}, dimensions={0}, use_global_device_ids=true | all-gather | bytes 40960 | tf_op jit(solution)/shard_map/all_gather | solution.py:12
  223.8 12.0 %pmax.23 = f32[2048]{0:T(1024)S(1)} all-reduce(f32[2048]{0:T(1024)S(1)} %add_reduce_fusion), channel_id=1, replica_groups=mesh['dp'=4,'cent'=8] {'cent'}, use_global_device_ids=true, to_apply=%region_21.22 | all-reduce | flops 2048 | bytes 16384 | tf_op jit(solution)/shard_map/pmax | solution.py:50
  235.9 7.7 %exponential_reduce_fusion = f32[2048]{0:T(1024)S(1)} fusion(f32[2048,2048]{1,0:T(8,128)} %get-tuple-element.141, f32[2048]{0:T(1024)S(1)} %pmax.23, f32[2048]{0:T(1024)S(1)} %add_subtract_fusion), kind=kLoop, calls=%fused_computation.15 | loop fusion | flops 12580864 | bytes 16801792 | tf_op jit(solution)/shard_map/reduce_sum | solution.py:51
  243.6 12.0 %psum.23 = f32[2048]{0:T(1024)S(1)} all-reduce(f32[2048]{0:T(1024)S(1)} %exponential_reduce_fusion), channel_id=1, replica_groups=mesh['dp'=4,'cent'=8] {'cent'}, use_global_device_ids=true, to_apply=%region_23.24 | all-reduce | flops 2048 | bytes 16384 | tf_op jit(solution)/shard_map/psum | solution.py:51
  255.7 8.0 %convert_reduce_fusion = (f32[2048]{0:T(1024)S(1)}, bf16[2048,2048]{1,0:T(8,128)(2,1)S(1)}) fusion(f32[2048]{0:T(1024)S(1)} %add_subtract_fusion, f32[2048,2048]{1,0:T(8,128)} %get-tuple-element.141, f32[2048]{0:T(1024)S(1)} %add_negate_fusion), kind=kLoop, calls=%fused_computation.13 | loop fusion | flops 20969472 | bytes 25190400 | tf_op jit(solution)/shard_map/reduce_sum | solution.py:57
  263.6 9.0 %fusion.8 = f32[2048,768]{1,0:T(8,128)} fusion(bf16[2048,2048]{1,0:T(8,128)(2,1)S(1)} %get-tuple-element.131, bf16[2048,768]{1,0:T(8,128)(2,1)S(1)} %copy-done), kind=kOutput, calls=%fused_computation.56 | convolution fusion | flops 6442450944 | bytes 17825792 | tf_op jit(solution)/shard_map/dot_general | solution.py:54
  273.9 12.4 %all-reduce = f32[2048]{0:T(1024)S(1)} all-reduce(f32[2048]{0:T(1024)S(1)} %get-tuple-element.130), channel_id=9, replica_groups=mesh['dp'=4,'cent'=8] {'dp'}, use_global_device_ids=true, to_apply=%region_26.27.clone | all-reduce | flops 2048 | bytes 16384
  286.5 97.8 %reduce-scatter.2.cloned.1.call-done = f32[512,768]{1,0:T(8,128)} async-done(((f32[2048,768]{1,0:T(8,128)}), f32[512,768]{1,0:T(8,128)}) %reduce-scatter.2.cloned.1.call-update) | async-done | bytes 1572880 | tf_op jit(solution)/shard_map/reduce_scatter | solution.py:59
  401.6 49.1 %all-gather.8.cloned.1.call-done = bf16[2048,768]{1,0:T(8,128)(2,1)} async-done(((bf16[512,768]{1,0:T(8,128)(2,1)}), bf16[2048,768]{1,0:T(8,128)(2,1)}) %all-gather.8.cloned.1.call-update) | async-done | bytes 3145744 | tf_op jit(solution)/shard_map/all_gather | solution.py:63
  462.8 12.6 %all-to-all-done.2 = bf16[8,64,768]{2,1,0:T(8,128)(2,1)} async-done(((bf16[8,64,768]{2,1,0:T(8,128)(2,1)}), bf16[8,64,768]{2,1,0:T(8,128)(2,1)}, u32[]{:S(2)}, u32[]{:S(2)}) %all-to-all-start.2) | async-done | bytes 786464 | tf_op jit(solution)/shard_map/all_to_all | solution.py:86
  (87 shorter events, 82.4 us)
Async XLA Ops:
  7.2 1.9 copy-start
  7.2 377.1 %reduce-scatter.2.cloned.1.call-start = ((), (), s32[]{:S(2)}) async-start(), calls=%async_computation.4 | async-start | bytes 7864320 | tf_op jit(solution)/shard_map/reduce_scatter | solution.py:59
  216.9 38.8 %copy-start.1 = (f32[2048]{0:T(1024)}, f32[2048]{0:T(1024)S(1)}, u32[]{:S(2)}) copy-start(f32[2048]{0:T(1024)S(1)} %add_subtract_fusion) | copy-start | bytes 24580
  255.6 17.0 %copy-start.2 = (f32[2048]{0:T(1024)}, f32[2048]{0:T(1024)S(1)}, u32[]{:S(2)}) copy-start(f32[2048]{0:T(1024)S(1)} %add_negate_fusion) | copy-start | bytes 24580
  263.6 9.1 %copy-start.4 = (u32[32]{0:T(128)S(1)}, u32[32]{0:T(128)}, u32[]{:S(2)}) copy-start(u32[32]{0:T(128)} %constant.77) | copy-start | bytes 388
  263.6 123.1 %copy-start.3 = (s32[256]{0:T(256)S(1)}, s32[256]{0:T(256)}, u32[]{:S(2)}) copy-start(s32[256]{0:T(256)} %param.11) | copy-start | bytes 3076
  272.6 178.1 %all-gather.8.cloned.1.call-start = ((), (), s32[]{:S(2)}) async-start(), calls=%async_computation.5 | async-start | bytes 3932160 | tf_op jit(solution)/shard_map/all_gather | solution.py:63
  389.0 8.3 %all-to-all-start.1 = ((s32[8,1,64]{2,1,0:T(1,128)}), s32[8,1,64]{2,1,0:T(1,128)S(1)}, u32[]{:S(2)}, u32[]{:S(2)}) async-start(s32[8,1,64]{2,1,0:T(1,128)} %all_to_all.15), calls=%async_computation.2 | async-start | bytes 8192 | tf_op jit(solution)/shard_map/all_to_all | solution.py:82
  397.3 58.8 %all-to-all-start = ((bf16[8,64,768]{2,1,0:T(8,128)(2,1)}), bf16[8,64,768]{2,1,0:T(8,128)(2,1)}, u32[]{:S(2)}, u32[]{:S(2)}) async-start(bf16[8,64,768]{2,1,0:T(8,128)(2,1)} %bitcast.30), calls=%async_computation.1 | async-start | bytes 1572864 | tf_op jit(solution)/shard_map/all_to_all | solution.py:81
  458.6 16.8 %all-to-all-start.2 = ((bf16[8,64,768]{2,1,0:T(8,128)(2,1)}), bf16[8,64,768]{2,1,0:T(8,128)(2,1)}, u32[]{:S(2)}, u32[]{:S(2)}) async-start(bf16[8,64,768]{2,1,0:T(8,128)(2,1)} %fusion), calls=%async_computation.3 | async-start | bytes 1572864 | tf_op jit(solution)/shard_map/all_to_all | solution.py:86
Sparse Core Ops, SparseCore 0:
  272.8 111.4 reduce-scatter.1
  386.9 63.8 all-gather.7
where the time goes:
time: 491 us; the launch traced here: 489 us
  blocking collectives  166 us (34%)
  waiting for transfers between devices  162 us (33%)
  other arithmetic  94.2 us (19%)
  matrix products  20.4 us (4%)
  local copies, waits for them, and re-layouts  20 us (4%)
  between operations  15 us (3%)
  starting transfers between devices  12.2 us (2%)
    reduce_scatter x1, waiting for transfers between devices, on_device(): lax.psum_scatter(numerator, 'dp', scatter_dimension=0, tiled=True)  97.8 us
    all_gather x6, blocking collectives, merged(): pieces = jax.tree.map(lambda part: lax.all_gather(part, axis), value)  80.6 us
    all_gather x1, waiting for transfers between devices, on_device(): updated = lax.all_gather(share_rows, 'dp', axis=0, tiled=True)  49.1 us
    psum x3, blocking collectives, on_device(): lax.psum(jnp.sum(jnp.exp(shifted - row_peak[:, None]), axis=1), 'cent')  36.3 us
    pmax x3, blocking collectives, on_device(): row_peak = lax.pmax(jnp.max(shifted, axis=1), 'cent')  36.2 us
    reduce_sum x3, other arithmetic, local_pair(): jnp.sum(jnp.exp(shifted - jnp.expand_dims(highest, axis)), axis=axis)  23.3 us
    reduce_sum x3, other arithmetic, on_device(): jnp.sum(jnp.exp(shifted - row_peak[:, None]), axis=1)  23.1 us
    reduce_max x3, other arithmetic, on_device(): row_peak = lax.pmax(jnp.max(shifted, axis=1), 'cent')  20.8 us
  transfers between devices with their start and end apart: 5, of which 4 were waited for; matrix products, arithmetic and copies ran while one was open for 2% of the time, Pallas kernels for 0%

commit v1 on v0

--- a/solution.py
+++ b/solution.py
@@ -60,7 +60,10 @@
         lax.psum_scatter(mass, "dp", scatter_dimension=0, tiled=True),
     )
     share_rows = (share_numer / share_mass[:, None]).astype(jnp.bfloat16)
-    updated = lax.all_gather(share_rows, "dp", axis=0, tiled=True)
+    updated = jnp.concatenate(
+        jax.lax.all_to_all(jnp.stack([share_rows] * jax.lax.axis_size("dp"), axis=0), "dp", 0, 0),
+        axis=0,
+    )
     send_count = row_count // owner_count
     capacity = max(2, 2 * send_count // owner_count)
     sender_rows = lax.dynamic_slice_in_dim(

time: 491 us -> 518 us (1.055)
  waiting for transfers between devices: 162 us -> 178 us
    all_to_all x0 -> x1, waiting for transfers between devices: none -> 68.7 us  [on_device(): jax.lax.all_to_all(jnp.stack([share_rows] * jax.lax.axis_size('dp'), axis...]
    all_gather x1 -> x0, waiting for transfers between devices: 49.1 us -> none  [on_device(): updated = lax.all_gather(share_rows, 'dp', axis=0, tiled=True)]
    reduce_scatter x1, waiting for transfers between devices: 97.8 us -> 90.1 us  [on_device(): lax.psum_scatter(numerator, 'dp', scatter_dimension=0, tiled=True)]
    all_to_all x1, waiting for transfers between devices: 0.01 us -> 7.12 us  [on_device(): lax.all_to_all(outgoing, 'cent', split_axis=0, concat_axis=0, tiled=True)]
where the time goes in v1:
time: 518 us; the launch traced here: 516 us
  waiting for transfers between devices  178 us (34%)
  blocking collectives  168 us (32%)
  other arithmetic  94.2 us (18%)
  local copies, waits for them, and re-layouts  23.1 us (4%)
  matrix products  20.4 us (4%)
  starting transfers between devices  16.6 us (3%)
  between operations  15.1 us (3%)
    reduce_scatter x1, waiting for transfers between devices, on_device(): lax.psum_scatter(numerator, 'dp', scatter_dimension=0, tiled=True)  90.1 us
    all_gather x6, blocking collectives, merged(): pieces = jax.tree.map(lambda part: lax.all_gather(part, axis), value)  80.6 us
    all_to_all x1, waiting for transfers between devices, on_device(): jax.lax.all_to_all(jnp.stack([share_rows] * jax.lax.axis_size('dp'), axis...  68.7 us
    psum x3, blocking collectives, on_device(): lax.psum(jnp.sum(jnp.exp(shifted - row_peak[:, None]), axis=1), 'cent')  36.3 us
    pmax x3, blocking collectives, on_device(): row_peak = lax.pmax(jnp.max(shifted, axis=1), 'cent')  36.2 us
    reduce_sum x3, other arithmetic, local_pair(): jnp.sum(jnp.exp(shifted - jnp.expand_dims(highest, axis)), axis=axis)  23.3 us
    reduce_sum x3, other arithmetic, on_device(): jnp.sum(jnp.exp(shifted - row_peak[:, None]), axis=1)  23.1 us
    reduce_max x3, other arithmetic, on_device(): row_peak = lax.pmax(jnp.max(shifted, axis=1), 'cent')  20.8 us
  transfers between devices with their start and end apart: 5, of which 4 were waited for; matrix products, arithmetic and copies ran while one was open for 2% of the time, Pallas kernels for 0%

profile of v1, /device:TPU:0, one launch (start us, length us, event | category | flops | bytes accessed | tf_op | source)
XLA Modules:
  0.0 516.2 jit_solution(14550638761694796270)
XLA Ops:
  9.1 11.5 %fusion.7 = (f32[2048]{0:T(1024)S(1)}, f32[2048,2048]{1,0:T(8,128)}) fusion(bf16[2048,768]{1,0:T(8,128)(2,1)S(1)} %copy-done, bf16[2048,768]{1,0:T(8,128)(2,1)} %param.10), kind=kOutput, calls=%fused_computation.55 | convolution fusion | flops 6450837504 | bytes 23076864 | tf_op jit(solution)/shard_map/dot_general | solution.py:39
  20.5 8.1 %exponential_reduce_fusion.5 = f32[2048]{0:T(1024)S(1)} fusion(f32[2048,2048]{1,0:T(8,128)} %get-tuple-element.141, f32[2048]{0:T(1024)S(1)} %get-tuple-element.140), kind=kLoop, calls=%fused_computation.20 | loop fusion | flops 8386560 | bytes 16793600 | tf_op jit(solution)/shard_map/reduce_sum | solution.py:29
  28.6 14.8 %all-gather.1 = f32[8192]{0:T(1024)S(1)} all-gather(f32[2048]{0:T(1024)S(1)} %exponential_reduce_fusion.5), channel_id=3, replica_groups=mesh['dp'=4,'cent'=8] {'dp'}, dimensions={0}, use_global_device_ids=true | all-gather | bytes 40960 | tf_op jit(solution)/shard_map/all_gather | solution.py:12
  43.5 13.2 %all-gather = f32[8192]{0:T(1024)S(1)} all-gather(f32[2048]{0:T(1024)S(1)} %get-tuple-element.140), channel_id=2, replica_groups=mesh['dp'=4,'cent'=8] {'dp'}, dimensions={0}, use_global_device_ids=true | all-gather | bytes 40960 | tf_op jit(solution)/shard_map/all_gather | solution.py:12
  63.8 12.1 %pmax.21 = f32[2048]{0:T(1024)S(1)} all-reduce(f32[2048]{0:T(1024)S(1)} %add_reduce_fusion.4), channel_id=1, replica_groups=mesh['dp'=4,'cent'=8] {'cent'}, use_global_device_ids=true, to_apply=%region_5.6 | all-reduce | flops 2048 | bytes 16384 | tf_op jit(solution)/shard_map/pmax | solution.py:50
  75.9 7.7 %exponential_reduce_fusion.4 = f32[2048]{0:T(1024)S(1)} fusion(f32[2048,2048]{1,0:T(8,128)} %get-tuple-element.141, f32[2048]{0:T(1024)S(1)} %pmax.21, f32[2048]{0:T(1024)S(1)} %add_subtract_fusion.2), kind=kLoop, calls=%fused_computation.19 | loop fusion | flops 12580864 | bytes 16801792 | tf_op jit(solution)/shard_map/reduce_sum | solution.py:51
  83.6 12.1 %psum.21 = f32[2048]{0:T(1024)S(1)} all-reduce(f32[2048]{0:T(1024)S(1)} %exponential_reduce_fusion.4), channel_id=1, replica_groups=mesh['dp'=4,'cent'=8] {'cent'}, use_global_device_ids=true, to_apply=%region_7.8 | all-reduce | flops 2048 | bytes 16384 | tf_op jit(solution)/shard_map/psum | solution.py:51
  102.6 7.6 %exponential_reduce_fusion.3 = f32[2048]{0:T(1024)S(1)} fusion(f32[2048,2048]{1,0:T(8,128)} %get-tuple-element.141, f32[2048]{0:T(1024)S(1)} %add_reduce_fusion.3, f32[2048]{0:T(1024)S(1)} %add_negate_fusion.2), kind=kLoop, calls=%fused_computation.18 | loop fusion | flops 12580864 | bytes 16801792 | tf_op jit(solution)/shard_map/reduce_sum | solution.py:29
  110.3 13.1 %all-gather.2 = f32[8192]{0:T(1024)S(1)} all-gather(f32[2048]{0:T(1024)S(1)} %add_reduce_fusion.3), channel_id=4, replica_groups=mesh['dp'=4,'cent'=8] {'dp'}, dimensions={0}, use_global_device_ids=true | all-gather | bytes 40960 | tf_op jit(solution)/shard_map/all_gather | solution.py:12
  123.4 13.2 %all-gather.3 = f32[8192]{0:T(1024)S(1)} all-gather(f32[2048]{0:T(1024)S(1)} %exponential_reduce_fusion.3), channel_id=5, replica_groups=mesh['dp'=4,'cent'=8] {'dp'}, dimensions={0}, use_global_device_ids=true | all-gather | bytes 40960 | tf_op jit(solution)/shard_map/all_gather | solution.py:12
  143.8 12.0 %pmax.22 = f32[2048]{0:T(1024)S(1)} all-reduce(f32[2048]{0:T(1024)S(1)} %add_reduce_fusion.2), channel_id=1, replica_groups=mesh['dp'=4,'cent'=8] {'cent'}, use_global_device_ids=true, to_apply=%region_13.14 | all-reduce | flops 2048 | bytes 16384 | tf_op jit(solution)/shard_map/pmax | solution.py:50
  155.8 7.7 %exponential_reduce_fusion.2 = f32[2048]{0:T(1024)S(1)} fusion(f32[2048,2048]{1,0:T(8,128)} %get-tuple-element.141, f32[2048]{0:T(1024)S(1)} %pmax.22, f32[2048]{0:T(1024)S(1)} %add_subtract_fusion.1), kind=kLoop, calls=%fused_computation.17 | loop fusion | flops 12580864 | bytes 16801792 | tf_op jit(solution)/shard_map/reduce_sum | solution.py:51
  163.5 12.2 %psum.22 = f32[2048]{0:T(1024)S(1)} all-reduce(f32[2048]{0:T(1024)S(1)} %exponential_reduce_fusion.2), channel_id=1, replica_groups=mesh['dp'=4,'cent'=8] {'cent'}, use_global_device_ids=true, to_apply=%region_15.16 | all-reduce | flops 2048 | bytes 16384 | tf_op jit(solution)/shard_map/psum | solution.py:51
  190.3 13.1 %all-gather.4 = f32[8192]{0:T(1024)S(1)} all-gather(f32[2048]{0:T(1024)S(1)} %add_reduce_fusion.1), channel_id=6, replica_groups=mesh['dp'=4,'cent'=8] {'dp'}, dimensions={0}, use_global_device_ids=true | all-gather | bytes 40960 | tf_op jit(solution)/shard_map/all_gather | solution.py:12
  203.4 13.2 %all-gather.5 = f32[8192]{0:T(1024)S(1)} all-gather(f32[2048]{0:T(1024)S(1)} %exponential_reduce_fusion.1), channel_id=7, replica_groups=mesh['dp'=4,'cent'=8] {'dp'}, dimensions={0}, use_global_device_ids=true | all-gather | bytes 40960 | tf_op jit(solution)/shard_map/all_gather | solution.py:12
  223.8 12.0 %pmax.23 = f32[2048]{0:T(1024)S(1)} all-reduce(f32[2048]{0:T(1024)S(1)} %add_reduce_fusion), channel_id=1, replica_groups=mesh['dp'=4,'cent'=8] {'cent'}, use_global_device_ids=true, to_apply=%region_21.22 | all-reduce | flops 2048 | bytes 16384 | tf_op jit(solution)/shard_map/pmax | solution.py:50
  235.9 7.7 %exponential_reduce_fusion = f32[2048]{0:T(1024)S(1)} fusion(f32[2048,2048]{1,0:T(8,128)} %get-tuple-element.141, f32[2048]{0:T(1024)S(1)} %pmax.23, f32[2048]{0:T(1024)S(1)} %add_subtract_fusion), kind=kLoop, calls=%fused_computation.15 | loop fusion | flops 12580864 | bytes 16801792 | tf_op jit(solution)/shard_map/reduce_sum | solution.py:51
  243.6 12.0 %psum.23 = f32[2048]{0:T(1024)S(1)} all-reduce(f32[2048]{0:T(1024)S(1)} %exponential_reduce_fusion), channel_id=1, replica_groups=mesh['dp'=4,'cent'=8] {'cent'}, use_global_device_ids=true, to_apply=%region_23.24 | all-reduce | flops 2048 | bytes 16384 | tf_op jit(solution)/shard_map/psum | solution.py:51
  255.7 8.0 %convert_reduce_fusion = (f32[2048]{0:T(1024)S(1)}, bf16[2048,2048]{1,0:T(8,128)(2,1)S(1)}) fusion(f32[2048]{0:T(1024)S(1)} %add_subtract_fusion, f32[2048,2048]{1,0:T(8,128)} %get-tuple-element.141, f32[2048]{0:T(1024)S(1)} %add_negate_fusion), kind=kLoop, calls=%fused_computation.13 | loop fusion | flops 20969472 | bytes 25190400 | tf_op jit(solution)/shard_map/reduce_sum | solution.py:57
  263.6 9.0 %fusion.8 = f32[2048,768]{1,0:T(8,128)} fusion(bf16[2048,2048]{1,0:T(8,128)(2,1)S(1)} %get-tuple-element.131, bf16[2048,768]{1,0:T(8,128)(2,1)S(1)} %copy-done), kind=kOutput, calls=%fused_computation.56 | convolution fusion | flops 6442450944 | bytes 17825792 | tf_op jit(solution)/shard_map/dot_general | solution.py:54
  279.5 15.0 %all-reduce = f32[2048]{0:T(1024)S(1)} all-reduce(f32[2048]{0:T(1024)S(1)} %get-tuple-element.130), channel_id=9, replica_groups=mesh['dp'=4,'cent'=8] {'dp'}, use_global_device_ids=true, to_apply=%region_26.27.clone | all-reduce | flops 2048 | bytes 16384
  294.6 90.1 %reduce-scatter.2.cloned.1.call-done = f32[512,768]{1,0:T(8,128)} async-done(((f32[2048,768]{1,0:T(8,128)}), f32[512,768]{1,0:T(8,128)}) %reduce-scatter.2.cloned.1.call-update) | async-done | bytes 1572880 | tf_op jit(solution)/shard_map/reduce_scatter | solution.py:59
  397.5 68.7 %all-to-all-done = bf16[4,512,768]{2,1,0:T(8,128)(2,1)} async-done(((bf16[4,512,768]{2,1,0:T(8,128)(2,1)}), bf16[4,512,768]{2,1,0:T(8,128)(2,1)}, u32[]{:S(2)}, u32[]{:S(2)}) %all-to-all-start) | async-done | bytes 3145760 | tf_op jit(solution)/shard_map/all_to_all | solution.py:64
  489.7 12.6 %all-to-all-done.3 = bf16[8,64,768]{2,1,0:T(8,128)(2,1)} async-done(((bf16[8,64,768]{2,1,0:T(8,128)(2,1)}), bf16[8,64,768]{2,1,0:T(8,128)(2,1)}, u32[]{:S(2)}, u32[]{:S(2)}) %all-to-all-start.3) | async-done | bytes 786464 | tf_op jit(solution)/shard_map/all_to_all | solution.py:89
  (87 shorter events, 94.9 us)
Async XLA Ops:
  7.2 1.9 copy-start
  7.2 377.5 %reduce-scatter.2.cloned.1.call-start = ((), (), s32[]{:S(2)}) async-start(), calls=%async_computation.5 | async-start | bytes 7864320 | tf_op jit(solution)/shard_map/reduce_scatter | solution.py:59
  216.9 38.8 %copy-start.1 = (f32[2048]{0:T(1024)}, f32[2048]{0:T(1024)S(1)}, u32[]{:S(2)}) copy-start(f32[2048]{0:T(1024)S(1)} %add_subtract_fusion) | copy-start | bytes 24580
  255.6 17.0 %copy-start.2 = (f32[2048]{0:T(1024)}, f32[2048]{0:T(1024)S(1)}, u32[]{:S(2)}) copy-start(f32[2048]{0:T(1024)S(1)} %add_negate_fusion) | copy-start | bytes 24580
  263.6 9.0 %copy-start.3 = (s32[256]{0:T(256)S(1)}, s32[256]{0:T(256)}, u32[]{:S(2)}) copy-start(s32[256]{0:T(256)} %param.11) | copy-start | bytes 3076
  263.6 14.6 %copy-start.4 = (u32[32]{0:T(128)S(1)}, u32[32]{0:T(128)}, u32[]{:S(2)}) copy-start(u32[32]{0:T(128)} %constant.77) | copy-start | bytes 388
  274.9 112.1 %all-to-all-start.2 = ((s32[8,1,64]{2,1,0:T(1,128)}), s32[8,1,64]{2,1,0:T(1,128)S(1)}, u32[]{:S(2)}, u32[]{:S(2)}) async-start(s32[8,1,64]{2,1,0:T(1,128)} %all_to_all.19), calls=%async_computation.3 | async-start | bytes 8192 | tf_op jit(solution)/shard_map/all_to_all | solution.py:85
  390.1 76.1 %all-to-all-start = ((bf16[4,512,768]{2,1,0:T(8,128)(2,1)}), bf16[4,512,768]{2,1,0:T(8,128)(2,1)}, u32[]{:S(2)}, u32[]{:S(2)}) async-start(bf16[4,512,768]{2,1,0:T(8,128)(2,1)} %stack.2), calls=%async_computation.1 | async-start | bytes 6291456 | tf_op jit(solution)/shard_map/all_to_all | solution.py:64
  466.2 16.8 %all-to-all-start.1 = ((bf16[8,64,768]{2,1,0:T(8,128)(2,1)}), bf16[8,64,768]{2,1,0:T(8,128)(2,1)}, u32[]{:S(2)}, u32[]{:S(2)}) async-start(bf16[8,64,768]{2,1,0:T(8,128)(2,1)} %bitcast.31), calls=%async_computation.2 | async-start | bytes 1572864 | tf_op jit(solution)/shard_map/all_to_all | solution.py:84
  485.5 16.8 %all-to-all-start.3 = ((bf16[8,64,768]{2,1,0:T(8,128)(2,1)}), bf16[8,64,768]{2,1,0:T(8,128)(2,1)}, u32[]{:S(2)}, u32[]{:S(2)}) async-start(bf16[8,64,768]{2,1,0:T(8,128)(2,1)} %fusion), calls=%async_computation.4 | async-start | bytes 1572864 | tf_op jit(solution)/shard_map/all_to_all | solution.py:89
Sparse Core Ops, SparseCore 0:
  272.8 111.8 reduce-scatter.1
